TPU v7x, 32 devices: a whole 2x2x4 slice. The times are simulated.
32 devices in a mesh: dp: 32 (over z, y, x, core), mp: 1.
Axes of the slice: x: 2, y: 2, z: 4, core: 2. Of those that a mesh axis runs over, the one named last changes fastest.
Arguments:
- candidates: bfloat16 [32768, 256], P('dp', 'mp'), may hold values from 0 to 1, as said below
- first_weight: bfloat16 [256, 4096], P(None, 'mp'), may hold values from -48 to 48
- first_bias: bfloat16 [1, 4096], P(None, 'mp'), may hold values from -3 to 3
- second_weight: bfloat16 [4096, 4096], P(None, 'mp'), may hold values from -0.09375 to 0.09375
- second_bias: float32 [4096], P('mp'), may hold values from -3 to 3
- head_weight: float32 [4096], P('mp'), may hold values from -0.09375 to 0.09375
- owners: int32 [1024, 1], P('dp'), may hold values from 0 to 31; in each aligned block of 32 rows (0 to 31, 32 to 63, ...) at most 2 rows name the same one
Outputs:
- collected: bfloat16 [2048, 32, 256], P('dp', None, 'mp')
- collected_scores: bfloat16 [2048, 32], P('dp')
Inputs may be any that keep to these rules, and one draw needn't show every extreme that they name: `candidates`: each row is nonnegative and sums to one. `owners`: among the 32 blocks of one index of dp no collector is named more than 2 times, a bound that some block reaches.
All inputs are finite; a program needn't handle non-finite values.
Results may differ from a plain program's by a relative error of at most 0.0033.
Values may be sent and summed in bfloat16 or wider, within the bound.
No kernel may reach another device: no remote copies, remote signals or barrier semaphores. Data moves between devices by JAX's collectives and lax.ppermute only.
A program may use at most 128 MiB of HBM per device.

v0:
```python
import functools

import jax
import jax.numpy as jnp
from jax import lax
from jax.experimental import pallas as pl
from jax.experimental.pallas import tpu as pltpu
from jax.sharding import PartitionSpec as P


BROWS = 32
PAIR = 2
LANES = 128
VMEM_GRANT = 44 << 20
FIRST_STEPS = 2
UNROLL = 3


def route_kernel(
    list_hbm, x_hbm, w1_hbm, b1_hbm, b2_hbm, head_hbm, row_hbm,
    out_hbm, x_ref, w1_ref, b1_ref, b2_ref, head_ref, row_ref,
    placed_ref, owners_ref, source_ref, list_sem, in_sems, out_sems,
):
    parts = out_sems.shape[0]
    slot_count = placed_ref.shape[0]
    block_count = owners_ref.shape[0]
    copies = [
        pltpu.make_async_copy(a, b, in_sems.at[i])
        for i, (a, b) in enumerate(
            (
                (x_hbm, x_ref), (w1_hbm, w1_ref), (b1_hbm, b1_ref), (b2_hbm, b2_ref), (head_hbm, head_ref),
                (row_hbm, row_ref),
            )
        )
    ]
    owner_copy = pltpu.make_async_copy(list_hbm, owners_ref, list_sem)
    owner_copy.start()
    for copy in copies:
        copy.start()
    for s in range(slot_count):
        source_ref[s] = -1
    owner_copy.wait()
    for b in range(block_count):
        first = owners_ref[b] * PAIR
        slot = first + jnp.where(source_ref[first] >= 0, 1, 0)
        source_ref[slot] = b
    copies[0].wait()

    def place(s, carry):
        source = source_ref[s]
        rows = x_ref[pl.ds(pl.multiple_of(jnp.maximum(source, 0) * BROWS, BROWS), BROWS), :]
        placed_ref[s] = jnp.where(source >= 0, rows, jnp.zeros_like(rows))
        return carry

    size = slot_count // parts
    stores = []
    for i in range(parts):
        lax.fori_loop(i * size, (i + 1) * size, place, 0, unroll=16)
        at = pl.ds(i * size, size)
        store = pltpu.make_async_copy(placed_ref.at[at], out_hbm.at[at], out_sems.at[i])
        store.start()
        stores.append(store)
    for copy in stores + copies[1:]:
        copy.wait()


def route(owners, kept, collectors):
    candidates = kept[0]
    rows, width = candidates.shape
    slots = collectors * PAIR
    parts = 2 if slots % 32 == 0 else 1
    hbm = pl.BlockSpec(memory_space=pltpu.HBM)
    vmem = pl.BlockSpec(memory_space=pltpu.VMEM)
    return pl.pallas_call(
        route_kernel,
        out_shape=[jax.ShapeDtypeStruct((slots, BROWS, width), candidates.dtype)]
        + [pltpu.VMEM(a.shape, a.dtype) for a in kept],
        in_specs=[hbm] * (1 + len(kept)),
        out_specs=[hbm] + [vmem] * len(kept),
        scratch_shapes=[
            pltpu.VMEM((slots, BROWS, width), candidates.dtype),
            pltpu.SMEM((rows // BROWS,), jnp.int32),
            pltpu.SMEM((slots,), jnp.int32),
            pltpu.SemaphoreType.DMA,
            pltpu.SemaphoreType.DMA((len(kept),)),
            pltpu.SemaphoreType.DMA((parts,)),
        ],
        name="route",
    )(owners[:, 0], *kept)


def score_kernel(
    x_ref, w1_ref, b1_ref, b2_ref, head_ref, owners_ref, w2_hbm, out_ref,
    w2_ref, hidden_ref, sums_ref, chooser_ref, w2_sem, *, tile_m, tile_h, singles, unroll,
):
    rows = x_ref.shape[0]
    width = w1_ref.shape[1]
    slots, _, tile_n = w2_ref.shape
    tiles = w2_hbm.shape[1] // tile_n
    blocks = rows // BROWS
    collectors = out_ref.shape[0]

    def load(j):
        at = pl.ds(pl.multiple_of(j * tile_n, tile_n), tile_n)
        return pltpu.make_async_copy(w2_hbm.at[:, at], w2_ref.at[j % slots], w2_sem.at[j % slots])

    load(0).start()

    sums_ref[...] = jnp.zeros_like(sums_ref)

    def first_layer(i, carry):
        for q in range(width // tile_h // FIRST_STEPS):
            start = pl.multiple_of(i * (width // FIRST_STEPS) + q * tile_h, tile_h)
            at = pl.ds(start, tile_h)
            first = jnp.dot(x_ref[...], w1_ref[:, at], preferred_element_type=jnp.float32)
            first = first + b1_ref[:, at].astype(jnp.float32)
            hidden_ref[:, at] = jnp.maximum(first, 0.0).astype(jnp.bfloat16)
        return carry

    lax.fori_loop(0, FIRST_STEPS, first_layer, 0)

    owner_row = jnp.broadcast_to(owners_ref[...], (blocks, blocks)).astype(jnp.float32)
    same_owner = owner_row == jnp.transpose(owner_row)
    before = lax.broadcasted_iota(jnp.int32, (blocks, blocks), 0) < lax.broadcasted_iota(
        jnp.int32, (blocks, blocks), 1
    )
    rank = jnp.sum(jnp.where(same_owner & before, 1.0, 0.0), axis=0, keepdims=True)
    target = owner_row[:1] * PAIR + rank
    for k in range(PAIR):
        slot = lax.broadcasted_iota(jnp.int32, (collectors, blocks), 0) * PAIR + k
        chooser_ref[k] = jnp.where(slot.astype(jnp.float32) == target, 1.0, 0.0).astype(jnp.bfloat16)

    def products(j):
        columns_at = pl.ds(pl.multiple_of(j * tile_n, tile_n), tile_n)
        for m in range(rows // tile_m):
            at = pl.ds(m * tile_m, tile_m)
            second = jnp.dot(hidden_ref[at, :], w2_ref[j % slots], preferred_element_type=jnp.float32)
            weighted = jnp.maximum(second + b2_ref[:, columns_at], 0.0) * head_ref[:, columns_at]
            total = weighted[:, :LANES]
            for q in range(1, tile_n // LANES):
                total = total + weighted[:, q * LANES:(q + 1) * LANES]
            sums_ref[at, :] += total

    def single(j, carry):
        load(j).wait()

        @pl.when(j + 1 < tiles)
        def _():
            load(j + 1).start()

        @pl.when(j == singles - 1)
        def _():
            for u in range(1, min(unroll, tiles - singles)):
                load(j + 1 + u).start()

        products(j)
        return carry

    def several(g, carry):
        base = singles + g * unroll
        for u in range(unroll):
            load(base + u).wait()

        @pl.when(base + unroll < tiles)
        def _():
            for u in range(unroll):
                load(base + unroll + u).start()

        for u in range(unroll):
            products(base + u)
        return carry

    lax.fori_loop(0, singles, single, 0)
    lax.fori_loop(0, (tiles - singles) // unroll, several, 0)

    scores = jnp.sum(sums_ref[...].reshape(blocks, BROWS, LANES), axis=2)
    rounded = scores.astype(jnp.bfloat16)
    for k in range(PAIR):
        placed = jnp.dot(chooser_ref[k], rounded, preferred_element_type=jnp.float32)
        out_ref[:, k, :] = placed.astype(out_ref.dtype)


def score(kept, second_weight, collectors):
    candidates, first_weight = kept[:2]
    rows, domains = candidates.shape
    width = first_weight.shape[1]
    outs = second_weight.shape[1]
    blocks = rows // BROWS
    tile_n, tile_m, tile_h, unroll = 512, 512, 512, UNROLL
    slots = 2 * unroll
    tiles = outs // tile_n
    singles = min(tiles, unroll - 1 + (tiles - unroll + 1) % unroll)
    return pl.pallas_call(
        functools.partial(score_kernel, tile_m=tile_m, tile_h=tile_h, singles=singles, unroll=unroll),
        out_shape=jax.ShapeDtypeStruct((collectors, PAIR, BROWS), jnp.bfloat16),
        in_specs=[pl.BlockSpec(memory_space=pltpu.VMEM)] * len(kept) + [pl.BlockSpec(memory_space=pltpu.HBM)],
        out_specs=pl.BlockSpec(memory_space=pltpu.VMEM),
        scratch_shapes=[
            pltpu.VMEM((slots, width, tile_n), second_weight.dtype),
            pltpu.VMEM((rows, width), jnp.bfloat16),
            pltpu.VMEM((rows, LANES), jnp.float32),
            pltpu.VMEM((PAIR, collectors, blocks), jnp.bfloat16),
            pltpu.SemaphoreType.DMA((slots,)),
        ],
        compiler_params=pltpu.CompilerParams(vmem_limit_bytes=VMEM_GRANT),
        cost_estimate=pl.CostEstimate(
            flops=2 * rows * width * (domains + outs),
            transcendentals=0,
            bytes_accessed=2 * (rows * domains + domains * width + width * outs),
        ),
        name="score",
    )(*kept, second_weight)


def settle_kernel(arrived_hbm, out_hbm, buffer_ref, in_sems, out_sems):
    parts = in_sems.shape[0]
    size = arrived_hbm.shape[0] // parts
    slices = [pl.ds(i * size, size) for i in range(parts)]
    fetches = [pltpu.make_async_copy(arrived_hbm.at[at], buffer_ref.at[at], in_sems.at[i]) for i, at in enumerate(slices)]
    stores = [pltpu.make_async_copy(buffer_ref.at[at], out_hbm.at[at], out_sems.at[i]) for i, at in enumerate(slices)]
    for fetch in fetches:
        fetch.start()
    for fetch, store in zip(fetches, stores):
        fetch.wait()
        store.start()
    for store in stores:
        store.wait()


def settle(arrived):
    parts = 4 if arrived.shape[0] % 4 == 0 else 1
    return pl.pallas_call(
        settle_kernel,
        out_shape=jax.ShapeDtypeStruct(arrived.shape, arrived.dtype),
        in_specs=[pl.BlockSpec(memory_space=pltpu.HBM)],
        out_specs=pl.BlockSpec(memory_space=pltpu.HBM),
        scratch_shapes=[
            pltpu.VMEM(arrived.shape, arrived.dtype),
            pltpu.SemaphoreType.DMA((parts,)),
            pltpu.SemaphoreType.DMA((parts,)),
        ],
        name="settle",
    )(arrived)


def local(candidates, first_weight, first_bias, second_weight, second_bias, head_weight, owners):
    if lax.axis_size("mp") > 1:
        return split_local(
            candidates, first_weight, first_bias, second_weight, second_bias, head_weight, owners
        )
    collectors = lax.axis_size("dp")
    width = candidates.shape[1]
    kept = (
        candidates, first_weight, first_bias, second_bias.reshape(1, -1), head_weight.reshape(1, -1),
        owners.reshape(1, -1),
    )
    outgoing, *kept = route(owners, kept, collectors)
    outgoing = outgoing.reshape(collectors, PAIR, BROWS, width)
    arrived = lax.all_to_all(outgoing, "dp", split_axis=0, concat_axis=0, tiled=True)
    outgoing_scores = score(kept, second_weight, collectors)
    arrived, outgoing_scores = lax.optimization_barrier((arrived, outgoing_scores))
    arrived_scores = lax.all_to_all(outgoing_scores, "dp", split_axis=0, concat_axis=0, tiled=True)
    collected = settle(arrived.reshape(collectors * PAIR, BROWS, width))
    return (
        collected,
        arrived_scores.reshape(collectors * PAIR, BROWS),
    )


def split_local(candidates, first_weight, first_bias, second_weight, second_bias, head_weight, owners):
    slice_width = candidates.shape[1]
    full_rows = lax.all_gather(candidates, "mp", axis=1, tiled=True)
    first_local = jnp.dot(
        full_rows, first_weight, preferred_element_type=jnp.float32
    ) + first_bias.astype(jnp.float32)
    hidden = jnp.maximum(first_local, 0.0).astype(jnp.bfloat16)
    second = jnp.dot(
        lax.all_gather(hidden, "mp", axis=1, tiled=True),
        second_weight,
        preferred_element_type=jnp.float32,
    )
    hidden_two = jnp.maximum(second + second_bias, 0.0)
    partial_score = jnp.dot(hidden_two, head_weight, precision=lax.Precision.HIGHEST)
    scores = lax.psum(partial_score, "mp")
    block_count = owners.shape[0]
    collectors = lax.axis_size("dp")
    owner_list = owners[:, 0]
    same_owner = owner_list[:, None] == owner_list[None, :]
    before = lax.broadcasted_iota(jnp.int32, (block_count, block_count), 0) < lax.broadcasted_iota(
        jnp.int32, (block_count, block_count), 1
    )
    earlier_count = jnp.sum(jnp.where(same_owner & before, 1, 0), axis=0).astype(jnp.int32)
    target = owner_list * PAIR + earlier_count
    slot_index = jnp.arange(collectors * PAIR, dtype=jnp.int32)
    chooser = slot_index[:, None] == target[None, :]
    block_rows = candidates.reshape(block_count, BROWS * slice_width)
    outgoing = jnp.dot(chooser.astype(jnp.bfloat16), block_rows, preferred_element_type=jnp.float32)
    outgoing = outgoing.astype(jnp.bfloat16).reshape(collectors, PAIR, BROWS, slice_width)
    score_blocks = scores.reshape(block_count, BROWS)
    outgoing_scores = jnp.dot(
        chooser.astype(jnp.float32), score_blocks, precision=lax.Precision.HIGHEST
    )
    outgoing_scores = outgoing_scores.astype(jnp.bfloat16).reshape(collectors, PAIR, BROWS)
    arrived, arrived_scores = (
        lax.all_to_all(outgoing, "dp", split_axis=0, concat_axis=0, tiled=True),
        lax.all_to_all(outgoing_scores, "dp", split_axis=0, concat_axis=0, tiled=True),
    )
    collected = arrived.reshape(collectors * PAIR, BROWS, slice_width)
    collected_scores = arrived_scores.reshape(collectors * PAIR, BROWS)
    return (collected, collected_scores)


def solution(mesh):
    placed = (
        P("dp", "mp"),
        P(None, "mp"),
        P(None, "mp"),
        P(None, "mp"),
        P("mp"),
        P("mp"),
        P("dp", None),
    )
    return jax.shard_map(
        local,
        mesh=mesh,
        in_specs=placed,
        out_specs=(P("dp", None, "mp"), P("dp", None)),
        check_vma=False,
    )
```

profile of v0, /device:TPU:0, one launch (start us, length us, event | category | flops | bytes accessed | tf_op | source)
XLA Modules:
  0.0 63.6 jit_solution(8963019003517387882)
XLA Ops:
  0.6 2.2 %route.1 = (bf16[64,32,256]{2,1,0:T(8,128)(2,1)}, bf16[1024,256]{1,0:T(8,128)(2,1)S(1)}, bf16[256,4096]{1,0:T(8,128)(2,1)S(1)}, bf16[1,4096]{1,0:T(2,128)(2,1)S(...) custom-call(s32[32]{0:T(128)} %bitcast.11, bf16[1024,256]{1,0:T(8,128)(2,1)} %x_hbm.1, ...), custom_call_target="tpu_custom_call" | custom-call | tf_op jit(solution)/shard_map/route/pallas_call | solution.py:74
  2.8 7.5 %all-to-all-start = ((bf16[32,2,32,256]{3,2,1,0:T(8,128)(2,1)}), bf16[32,2,32,256]{3,2,1,0:T(8,128)(2,1)}, u32[]{:S(2)}, u32[]{:S(2)}) async-start(bf16[32,2,32,256]{3,2,1,0:T(8,128)(2,1)} %bitcast.7), calls=%async_computation | async-start | bytes 2097152 | tf_op jit(solution)/shard_map/all_to_all | solution.py:259
  10.3 39.6 %score.1 = bf16[32,2,32]{2,1,0:T(2,128)(2,1)} custom-call(bf16[1024,256]{1,0:T(8,128)(2,1)S(1)} %get-tuple-element.12.x_ref, bf16[256,4096]{1,0:T(8,128)(2,1)S(1)} %get-tuple-element.13.w1_ref, bf16[1,4096]{1,0:T(2,128)(2,1)S(1)} %get-tuple-element.14.b1_ref, f32[1,4096]{1,0:T(1,128)S(1)} %get-tuple-element.15.b2_ref, ...), custom_call_target="tpu_custom_call" | custom-call | flops 36507222016 | bytes 36175872 | tf_op jit(solution)/shard_map/score/pallas_call | solution.py:193
  49.9 0.0 all-to-all-done
  49.9 5.8 %all-to-all-start.1 = ((bf16[32,2,32]{2,1,0:T(2,128)(2,1)}), bf16[32,2,32]{2,1,0:T(2,128)(2,1)S(1)}, u32[]{:S(2)}, u32[]{:S(2)}) async-start(bf16[32,2,32]{2,1,0:T(2,128)(2,1)} %score.1), calls=%async_computation.1 | async-start | bytes 32768 | tf_op jit(solution)/shard_map/all_to_all | solution.py:262
  55.7 2.0 %settle.1 = bf16[64,32,256]{2,1,0:T(8,128)(2,1)} custom-call(bf16[64,32,256]{2,1,0:T(8,128)(2,1)} %bitcast.5.arrived_hbm), custom_call_target="tpu_custom_call" | custom-call | tf_op jit(solution)/shard_map/settle/pallas_call | solution.py:232
  57.7 5.2 %all-to-all-done.1 = bf16[32,2,32]{2,1,0:T(2,128)(2,1)S(1)} async-done(((bf16[32,2,32]{2,1,0:T(2,128)(2,1)}), bf16[32,2,32]{2,1,0:T(2,128)(2,1)S(1)}, u32[]{:S(2)}, u32[]{:S(2)}) %all-to-all-start.1) | async-done | bytes 4128 | tf_op jit(solution)/shard_map/all_to_all | solution.py:262
  62.9 0.7 %copy.9 = bf16[64,32]{0,1:T(8,128)(2,1)} copy(bf16[64,32]{1,0:T(8,128)(2,1)S(1)} %bitcast.8) | data formatting | bytes 8192
Async XLA Ops:
  2.8 47.1 %all-to-all-start = ((bf16[32,2,32,256]{3,2,1,0:T(8,128)(2,1)}), bf16[32,2,32,256]{3,2,1,0:T(8,128)(2,1)}, u32[]{:S(2)}, u32[]{:S(2)}) async-start(bf16[32,2,32,256]{3,2,1,0:T(8,128)(2,1)} %bitcast.7), calls=%async_computation | async-start | bytes 2097152 | tf_op jit(solution)/shard_map/all_to_all | solution.py:259
  49.9 13.0 %all-to-all-start.1 = ((bf16[32,2,32]{2,1,0:T(2,128)(2,1)}), bf16[32,2,32]{2,1,0:T(2,128)(2,1)S(1)}, u32[]{:S(2)}, u32[]{:S(2)}) async-start(bf16[32,2,32]{2,1,0:T(2,128)(2,1)} %score.1), calls=%async_computation.1 | async-start | bytes 32768 | tf_op jit(solution)/shard_map/all_to_all | solution.py:262
where the time goes:
time: 63.8 us; the launch traced here: 63.6 us
  Pallas kernels  43.8 us (69%)
  starting transfers between devices  13.2 us (21%)
  waiting for transfers between devices  5.19 us (8%)
  local copies, waits for them, and re-layouts  0.68 us (1%)
  between operations  0.68 us (1%)
    pallas_call x1, Pallas kernels, score(): pl.pallas_call(functools.partial(score_kernel, tile_m=tile_m, tile_h=tile...  39.6 us
    all_to_all x1, starting transfers between devices, local(): lax.all_to_all(outgoing, 'dp', split_axis=0, concat_axis=0, tiled=True)  7.46 us
    all_to_all x1, starting transfers between devices, local(): lax.all_to_all(outgoing_scores, 'dp', split_axis=0, concat_axis=0, tiled=...  5.77 us
    all_to_all x1, waiting for transfers between devices, local(): lax.all_to_all(outgoing_scores, 'dp', split_axis=0, concat_axis=0, tiled=...  5.19 us
    pallas_call x1, Pallas kernels, route(): pl.pallas_call(route_kernel, out_shape=[jax.ShapeDtypeStruct((slots, BROW...  2.18 us
    pallas_call x1, Pallas kernels, settle(): pl.pallas_call(settle_kernel, out_shape=jax.ShapeDtypeStruct(arrived.shap...  1.98 us
  transfers between devices with their start and end apart: 2, of which 1 were waited for; matrix products, arithmetic and copies ran while one was open for 0% of the time, Pallas kernels for 65%

commit v1 on v0

--- a/solution.py
+++ b/solution.py
@@ -13,7 +13,7 @@
 LANES = 128
 VMEM_GRANT = 44 << 20
 FIRST_STEPS = 2
-UNROLL = 3
+UNROLL = 2
 
 
 def route_kernel(
@@ -55,7 +55,7 @@
     size = slot_count // parts
     stores = []
     for i in range(parts):
-        lax.fori_loop(i * size, (i + 1) * size, place, 0, unroll=16)
+        lax.fori_loop(i * size, (i + 1) * size, place, 0, unroll=8)
         at = pl.ds(i * size, size)
         store = pltpu.make_async_copy(placed_ref.at[at], out_hbm.at[at], out_sems.at[i])
         store.start()
@@ -68,7 +68,7 @@
     candidates = kept[0]
     rows, width = candidates.shape
     slots = collectors * PAIR
-    parts = 2 if slots % 32 == 0 else 1
+    parts = 4 if slots % 32 == 0 else 1
     hbm = pl.BlockSpec(memory_space=pltpu.HBM)
     vmem = pl.BlockSpec(memory_space=pltpu.VMEM)
     return pl.pallas_call(
@@ -108,6 +108,17 @@
 
     sums_ref[...] = jnp.zeros_like(sums_ref)
 
+    owner_row = jnp.broadcast_to(owners_ref[...], (blocks, blocks)).astype(jnp.float32)
+    same_owner = owner_row == jnp.transpose(owner_row)
+    before = lax.broadcasted_iota(jnp.int32, (blocks, blocks), 0) < lax.broadcasted_iota(
+        jnp.int32, (blocks, blocks), 1
+    )
+    rank = jnp.sum(jnp.where(same_owner & before, 1.0, 0.0), axis=0, keepdims=True)
+    target = owner_row[:1] * PAIR + rank
+    for k in range(PAIR):
+        slot = lax.broadcasted_iota(jnp.int32, (collectors, blocks), 0) * PAIR + k
+        chooser_ref[k] = jnp.where(slot.astype(jnp.float32) == target, 1.0, 0.0).astype(jnp.bfloat16)
+
     def first_layer(i, carry):
         for q in range(width // tile_h // FIRST_STEPS):
             start = pl.multiple_of(i * (width // FIRST_STEPS) + q * tile_h, tile_h)
@@ -118,17 +129,6 @@
         return carry
 
     lax.fori_loop(0, FIRST_STEPS, first_layer, 0)
-
-    owner_row = jnp.broadcast_to(owners_ref[...], (blocks, blocks)).astype(jnp.float32)
-    same_owner = owner_row == jnp.transpose(owner_row)
-    before = lax.broadcasted_iota(jnp.int32, (blocks, blocks), 0) < lax.broadcasted_iota(
-        jnp.int32, (blocks, blocks), 1
-    )
-    rank = jnp.sum(jnp.where(same_owner & before, 1.0, 0.0), axis=0, keepdims=True)
-    target = owner_row[:1] * PAIR + rank
-    for k in range(PAIR):
-        slot = lax.broadcasted_iota(jnp.int32, (collectors, blocks), 0) * PAIR + k
-        chooser_ref[k] = jnp.where(slot.astype(jnp.float32) == target, 1.0, 0.0).astype(jnp.bfloat16)
 
     def products(j):
         columns_at = pl.ds(pl.multiple_of(j * tile_n, tile_n), tile_n)

time: 63.8 us -> 63.9 us (level)
  no operation moved by 1% of the time
where the time goes in v1:
time: 63.9 us; the launch traced here: 63.6 us
  Pallas kernels  43.8 us (69%)
  starting transfers between devices  13.2 us (21%)
  waiting for transfers between devices  5.19 us (8%)
  local copies, waits for them, and re-layouts  0.68 us (1%)
  between operations  0.68 us (1%)
    pallas_call x1, Pallas kernels, score(): pl.pallas_call(functools.partial(score_kernel, tile_m=tile_m, tile_h=tile...  39.7 us
    all_to_all x1, starting transfers between devices, local(): lax.all_to_all(outgoing, 'dp', split_axis=0, concat_axis=0, tiled=True)  7.46 us
    all_to_all x1, starting transfers between devices, local(): lax.all_to_all(outgoing_scores, 'dp', split_axis=0, concat_axis=0, tiled=...  5.76 us
    all_to_all x1, waiting for transfers between devices, local(): lax.all_to_all(outgoing_scores, 'dp', split_axis=0, concat_axis=0, tiled=...  5.19 us
    pallas_call x1, Pallas kernels, route(): pl.pallas_call(route_kernel, out_shape=[jax.ShapeDtypeStruct((slots, BROW...  2.15 us
    pallas_call x1, Pallas kernels, settle(): pl.pallas_call(settle_kernel, out_shape=jax.ShapeDtypeStruct(arrived.shap...  1.98 us
  transfers between devices with their start and end apart: 2, of which 1 were waited for; matrix products, arithmetic and copies ran while one was open for 0% of the time, Pallas kernels for 65%

profile of v1, /device:TPU:0, one launch (start us, length us, event | category | flops | bytes accessed | tf_op | source)
XLA Modules:
  0.0 63.6 jit_solution(9563923335565051269)
XLA Ops:
  0.6 2.1 %route.1 = (bf16[64,32,256]{2,1,0:T(8,128)(2,1)}, bf16[1024,256]{1,0:T(8,128)(2,1)S(1)}, bf16[256,4096]{1,0:T(8,128)(2,1)S(1)}, bf16[1,4096]{1,0:T(2,128)(2,1)S(...) custom-call(s32[32]{0:T(128)} %bitcast.11, bf16[1024,256]{1,0:T(8,128)(2,1)} %x_hbm.1, ...), custom_call_target="tpu_custom_call" | custom-call | tf_op jit(solution)/shard_map/route/pallas_call | solution.py:74
  2.8 7.5 %all-to-all-start = ((bf16[32,2,32,256]{3,2,1,0:T(8,128)(2,1)}), bf16[32,2,32,256]{3,2,1,0:T(8,128)(2,1)}, u32[]{:S(2)}, u32[]{:S(2)}) async-start(bf16[32,2,32,256]{3,2,1,0:T(8,128)(2,1)} %bitcast.7), calls=%async_computation | async-start | bytes 2097152 | tf_op jit(solution)/shard_map/all_to_all | solution.py:259
  10.3 39.7 %score.1 = bf16[32,2,32]{2,1,0:T(2,128)(2,1)} custom-call(bf16[1024,256]{1,0:T(8,128)(2,1)S(1)} %get-tuple-element.12.x_ref, bf16[256,4096]{1,0:T(8,128)(2,1)S(1)} %get-tuple-element.13.w1_ref, bf16[1,4096]{1,0:T(2,128)(2,1)S(1)} %get-tuple-element.14.b1_ref, f32[1,4096]{1,0:T(1,128)S(1)} %get-tuple-element.15.b2_ref, ...), custom_call_target="tpu_custom_call" | custom-call | flops 36507222016 | bytes 36175872 | tf_op jit(solution)/shard_map/score/pallas_call | solution.py:193
  49.9 0.0 all-to-all-done
  50.0 5.8 %all-to-all-start.1 = ((bf16[32,2,32]{2,1,0:T(2,128)(2,1)}), bf16[32,2,32]{2,1,0:T(2,128)(2,1)S(1)}, u32[]{:S(2)}, u32[]{:S(2)}) async-start(bf16[32,2,32]{2,1,0:T(2,128)(2,1)} %score.1), calls=%async_computation.1 | async-start | bytes 32768 | tf_op jit(solution)/shard_map/all_to_all | solution.py:262
  55.7 2.0 %settle.1 = bf16[64,32,256]{2,1,0:T(8,128)(2,1)} custom-call(bf16[64,32,256]{2,1,0:T(8,128)(2,1)} %bitcast.5.arrived_hbm), custom_call_target="tpu_custom_call" | custom-call | tf_op jit(solution)/shard_map/settle/pallas_call | solution.py:232
  57.7 5.2 %all-to-all-done.1 = bf16[32,2,32]{2,1,0:T(2,128)(2,1)S(1)} async-done(((bf16[32,2,32]{2,1,0:T(2,128)(2,1)}), bf16[32,2,32]{2,1,0:T(2,128)(2,1)S(1)}, u32[]{:S(2)}, u32[]{:S(2)}) %all-to-all-start.1) | async-done | bytes 4128 | tf_op jit(solution)/shard_map/all_to_all | solution.py:262
  62.9 0.7 %copy.9 = bf16[64,32]{0,1:T(8,128)(2,1)} copy(bf16[64,32]{1,0:T(8,128)(2,1)S(1)} %bitcast.8) | data formatting | bytes 8192
Async XLA Ops:
  2.8 47.2 %all-to-all-start = ((bf16[32,2,32,256]{3,2,1,0:T(8,128)(2,1)}), bf16[32,2,32,256]{3,2,1,0:T(8,128)(2,1)}, u32[]{:S(2)}, u32[]{:S(2)}) async-start(bf16[32,2,32,256]{3,2,1,0:T(8,128)(2,1)} %bitcast.7), calls=%async_computation | async-start | bytes 2097152 | tf_op jit(solution)/shard_map/all_to_all | solution.py:259
  50.0 12.9 %all-to-all-start.1 = ((bf16[32,2,32]{2,1,0:T(2,128)(2,1)}), bf16[32,2,32]{2,1,0:T(2,128)(2,1)S(1)}, u32[]{:S(2)}, u32[]{:S(2)}) async-start(bf16[32,2,32]{2,1,0:T(2,128)(2,1)} %score.1), calls=%async_computation.1 | async-start | bytes 32768 | tf_op jit(solution)/shard_map/all_to_all | solution.py:262
